TPU v7x, 32 devices: a whole 2x2x4 slice. The times are simulated.
32 devices in a mesh: band: 8 (over z, core), grid: 4 (over y, x).
Axes of the slice: x: 2, y: 2, z: 4, core: 2. Of those that a mesh axis runs over, the one named last changes fastest.
Arguments:
- orbitals: float32 [8, 128, 128, 128], P('band', 'grid')
- sources: int32 [4], replicated, may hold values from 0 to 7, as said below
Outputs:
- compressed: float32 [8, 128, 128, 128], P(None, 'grid', 'band')
Inputs may be any that keep to these rules, and one draw needn't show every extreme that they name: `sources`: 4 distinct orbital indices in some order.
All inputs are finite; a program needn't handle non-finite values.
Results may differ from a plain program's by a relative error of at most 0.0003.
Values sent between devices are 32-bit elements; how exact they have to be, the bound alone decides.
A program may use at most 64 MiB of HBM per device.

v0:
```python
import math
import jax
import jax.numpy as jnp
from jax import lax
from jax.sharding import PartitionSpec as P

highest = lax.Precision.HIGHEST


def spread_2(block, axis, owner):
    block = jnp.where(lax.axis_index(axis) == owner, block, jnp.zeros_like(block))
    return lax.psum(block, axis)


def cas_table(length):
    index_values = jnp.arange(length, dtype=jnp.int32)
    products = index_values[:, None] * index_values[None, :] % length
    angles = products.astype(jnp.float32) * (2.0 * math.pi / length)
    return jnp.cos(angles) + jnp.sin(angles)


def squared_waves(start, count, length):
    index_values = start + jnp.arange(count, dtype=jnp.int32)
    signed = jnp.where(index_values < length // 2, index_values, index_values - length)
    waves = signed.astype(jnp.float32) * (2.0 * math.pi / length)
    return waves * waves


def per_device(orbitals, sources):
    band_count, slab_x, full_y, full_z = orbitals.shape
    grid_count = lax.axis_size("grid")
    full_x = slab_x * grid_count
    total_bands = band_count * lax.axis_size("band")
    round_count = sources.shape[0]
    table_x = cas_table(full_x)
    table_y = cas_table(full_y)
    table_z = cas_table(full_z)
    column_y = full_y // grid_count
    start_y = lax.axis_index("grid") * column_y
    waves = (
        squared_waves(0, full_x, full_x)[:, None, None]
        + squared_waves(start_y, column_y, full_y)[None, :, None]
        + squared_waves(0, full_z, full_z)[None, None, :]
    )
    screen = (4.0 * math.pi / full_x) ** 2
    volume = 1.0 / (full_x * full_y * full_z)
    kernel = volume / (waves + screen)

    def plane_transform(field):
        spread = jnp.einsum("bxyz,zk->bxyk", field, table_z, precision=highest)
        return jnp.einsum("bxyk,yj->bxjk", spread, table_y, precision=highest)

    def own_slab(number):
        owner = number // band_count
        local = number % band_count
        return (owner, lax.dynamic_index_in_dim(orbitals, local, 0, keepdims=False))

    def fetch(number):
        owner, slab = own_slab(number)
        return spread_2(slab, "band", owner)

    arrived = [fetch(sources[turn]) for turn in range(round_count)]
    terms = jnp.zeros(orbitals.shape, jnp.float32)
    for turn in range(round_count):
        source = arrived[turn][None]
        spectra = plane_transform(orbitals * source)
        potential_columns = lax.all_to_all(spectra, "grid", split_axis=2, concat_axis=1, tiled=True)
        line_spread = jnp.einsum("bxyz,xa->bayz", potential_columns, table_x, precision=highest)
        line_spread = line_spread * kernel[None]
        filtered = jnp.einsum("bayz,ax->bxyz", line_spread, table_x, precision=highest)
        terms = terms + source * plane_transform(
            lax.all_to_all(filtered, "grid", split_axis=1, concat_axis=2, tiled=True)
        )
    orbital_cols, term_cols = (
        lax.all_to_all(orbitals, "band", split_axis=2, concat_axis=0, tiled=True),
        lax.all_to_all(terms, "band", split_axis=2, concat_axis=0, tiled=True),
    )
    flat_orbitals = orbital_cols.reshape(total_bands, -1)
    flat_terms = term_cols.reshape(total_bands, -1)
    partial_intersection = (
        jnp.dot(flat_orbitals, flat_terms.T, precision=highest, preferred_element_type=jnp.float32)
        * volume
    )
    intersection = lax.psum(partial_intersection, ("band", "grid"))
    factor = jnp.linalg.cholesky(intersection)
    solved = lax.linalg.triangular_solve(factor, flat_terms, left_side=True, lower=True)
    return (-solved).reshape(term_cols.shape)


def solution(mesh):
    placed = (P("band", "grid", None, None), P())
    return jax.shard_map(
        per_device,
        mesh=mesh,
        in_specs=placed,
        out_specs=P(None, "grid", "band", None),
        check_vma=False,
    )
```

profile of v0, /device:TPU:10, one launch (start us, length us, event | category | flops | bytes accessed | tf_op | source)
XLA Modules:
  0.0 616.8 jit_solution(3678246858079370884)
XLA Ops:
  10.5 5.3 broadcast_select_fusion.3
  15.9 176.9 %all-reduce.3.cloned.1.call-done = (f32[1,32,128,128]{3,2,1,0:T(8,128)}, f32[1,32,128,128]{3,2,1,0:T(8,128)}, f32[1,32,128,128]{3,2,1,0:T(8,128)}, f32[1,32,128,128]{3,2,1,0:T(8,128)}) async-done(((f32[1,32,128,128]{3,2,1,0:T(8,128)}, f32[1,32,128,128]{3,2,1,0:T(8,128)}, f32[1,32,128,128]{3,2,1,0:T(8,128)}, f32[1,32,128,128]{3,2,1,0:T(8,128)}), (f32[1,32,128,128]{3,2,1,0:T(8,128)}, ...) | async-done | bytes 8388624 | tf_op jit(solution)/shard_map/psum | solution.py:12
  192.8 3.7 fusion.11
  201.2 5.2 all-to-all-start.2
  206.4 3.7 fusion.13
  214.9 15.8 %all-to-all-done.2 = f32[1,32,128,128]{3,1,0,2:T(8,128)} async-done(((f32[1,32,128,128]{3,1,0,2:T(8,128)}), f32[1,32,128,128]{3,1,0,2:T(8,128)}, u32[]{:S(2)}, u32[]{:S(2)}) %all-to-all-start.2) | async-done | bytes 2097184 | tf_op jit(solution)/shard_map/all_to_all | solution.py:67
  230.7 5.0 all-to-all-start
  235.7 3.7 fusion.9
  244.2 15.5 %all-to-all-done = f32[1,32,128,128]{3,1,0,2:T(8,128)} async-done(((f32[1,32,128,128]{3,1,0,2:T(8,128)}), f32[1,32,128,128]{3,1,0,2:T(8,128)}, u32[]{:S(2)}, u32[]{:S(2)}) %all-to-all-start) | async-done | bytes 2097184 | tf_op jit(solution)/shard_map/all_to_all | solution.py:67
  259.7 5.5 all-to-all-start.4
  265.2 3.7 fusion.7
  273.6 15.5 %all-to-all-done.4 = f32[1,32,128,128]{3,1,0,2:T(8,128)} async-done(((f32[1,32,128,128]{3,1,0,2:T(8,128)}), f32[1,32,128,128]{3,1,0,2:T(8,128)}, u32[]{:S(2)}, u32[]{:S(2)}) %all-to-all-start.4) | async-done | bytes 2097184 | tf_op jit(solution)/shard_map/all_to_all | solution.py:67
  289.0 5.0 all-to-all-start.6
  305.4 12.6 %all-to-all-done.6 = f32[1,32,128,128]{3,1,0,2:T(8,128)} async-done(((f32[1,32,128,128]{3,1,0,2:T(8,128)}), f32[1,32,128,128]{3,1,0,2:T(8,128)}, u32[]{:S(2)}, u32[]{:S(2)}) %all-to-all-start.6) | async-done | bytes 2097184 | tf_op jit(solution)/shard_map/all_to_all | solution.py:67
  318.0 5.2 all-to-all-start.3
  334.5 12.6 %all-to-all-done.3 = f32[1,128,32,128]{3,2,0,1:T(8,128)} async-done(((f32[1,128,32,128]{3,2,0,1:T(8,128)}), f32[1,128,32,128]{3,2,0,1:T(8,128)}, u32[]{:S(2)}, u32[]{:S(2)}) %all-to-all-start.3) | async-done | bytes 2097184 | tf_op jit(solution)/shard_map/all_to_all | solution.py:72
  347.1 5.2 all-to-all-start.1
  363.6 12.7 %all-to-all-done.1 = f32[1,128,32,128]{3,2,0,1:T(8,128)} async-done(((f32[1,128,32,128]{3,2,0,1:T(8,128)}), f32[1,128,32,128]{3,2,0,1:T(8,128)}, u32[]{:S(2)}, u32[]{:S(2)}) %all-to-all-start.1) | async-done | bytes 2097184 | tf_op jit(solution)/shard_map/all_to_all | solution.py:72
  376.3 5.5 all-to-all-start.5
  401.4 4.3 all-to-all-done.5
  405.7 5.1 all-to-all-start.7
  413.0 3.5 fusion.86
  418.7 3.5 fusion.91
  424.3 3.5 fusion.81
  427.8 6.8 %all-to-all-done.7 = f32[1,128,32,128]{3,2,0,1:T(8,128)} async-done(((f32[1,128,32,128]{3,2,0,1:T(8,128)}), f32[1,128,32,128]{3,2,0,1:T(8,128)}, u32[]{:S(2)}, u32[]{:S(2)}) %all-to-all-start.7) | async-done | bytes 2097184 | tf_op jit(solution)/shard_map/all_to_all | solution.py:72
  439.0 6.3 %fusion.3 = f32[1,32,128,128]{3,2,1,0:T(8,128)S(1)} fusion(f32[1,32,128,128]{3,2,1,0:T(8,128)S(1)} %copy-done.1, f32[1,32,128,128]{3,2,1,0:T(8,128)S(1)} %copy-done.2, f32[128,32,128]{2,0,1:T(8,128)} %fusion.81, f32[1,32,128,128]{3,2,1,0:T(8,128)S(1)} %copy-done.3, f32[128,32,128]{2,0,1:T(8,128)} %fusion.86, f32[1,32,128,128]{3,2,1,0:T(8,128)S(1)} %copy-done.4, ...), kind=kOutput, calls=%fused_computation.5 | convolution fusion | flops 809222144 | bytes 18874368 | tf_op jit(solution)/shard_map/bxyk,yj->bxjk/dot_general | solution.py:51
  447.8 4.8 all-to-all-start.8
  455.1 43.0 %all-to-all-done.8 = f32[1,32,128,128]{3,1,0,2:T(8,128)} async-done(((f32[1,32,128,128]{3,1,0,2:T(8,128)}), f32[1,32,128,128]{3,1,0,2:T(8,128)}, u32[]{:S(2)}, u32[]{:S(2)}) %all-to-all-start.8) | async-done | bytes 2097184 | tf_op jit(solution)/shard_map/all_to_all | solution.py:76
  498.2 8.1 %all-to-all-start.9 = ((f32[1,32,128,128]{3,1,0,2:T(8,128)}), f32[1,32,128,128]{3,1,0,2:T(8,128)}, u32[]{:S(2)}, u32[]{:S(2)}) async-start(f32[1,32,128,128]{3,1,0,2:T(8,128)} %copy.82), calls=%async_computation.9 | async-start | bytes 4194304 | tf_op jit(solution)/shard_map/all_to_all | solution.py:75
  509.1 42.7 %all-to-all-done.9 = f32[1,32,128,128]{3,1,0,2:T(8,128)} async-done(((f32[1,32,128,128]{3,1,0,2:T(8,128)}), f32[1,32,128,128]{3,1,0,2:T(8,128)}, u32[]{:S(2)}, u32[]{:S(2)}) %all-to-all-start.9) | async-done | bytes 2097184 | tf_op jit(solution)/shard_map/all_to_all | solution.py:75
  551.8 9.3 %fusion.57 = f32[8,8]{0,1:T(8,128)S(1)} fusion(f32[1,32,8,16,128]{4,1,3,2,0:T(8,128)} %bitcast.64, f32[1,32,8,16,128]{4,1,3,2,0:T(8,128)} %bitcast.61), kind=kOutput, calls=%fused_computation.51 | convolution fusion | flops 50331712 | bytes 4194560 | tf_op jit(solution)/shard_map/dot_general | solution.py:81
  561.1 42.1 %psum.39 = f32[8,8]{0,1:T(8,128)S(1)} all-reduce(f32[8,8]{0,1:T(8,128)S(1)} %fusion.57), channel_id=1, replica_groups=mesh['band'=8,'grid'=4] {'band','grid'}, use_global_device_ids=true, to_apply=%region_4.5 | all-reduce | flops 64 | bytes 512 | tf_op jit(solution)/shard_map/psum | solution.py:84
  (68 shorter events, 98.9 us)
Async XLA Ops:
  6.5 186.2 %all-reduce.3.cloned.1.call-start = ((), (), s32[]{:S(2)}) async-start(), calls=%async_computation.10 | async-start | bytes 16777216 | tf_op jit(solution)/shard_map/psum | solution.py:12
  15.9 176.9 %copy-start = (f32[1,32,128,128]{3,2,1,0:T(8,128)S(1)}, f32[1,32,128,128]{3,2,1,0:T(8,128)}, u32[]{:S(2)}) copy-start(f32[1,32,128,128]{3,2,1,0:T(8,128)} %param.2) | copy-start | bytes 6291460
  201.2 29.5 %all-to-all-start.2 = ((f32[1,32,128,128]{3,1,0,2:T(8,128)}), f32[1,32,128,128]{3,1,0,2:T(8,128)}, u32[]{:S(2)}, u32[]{:S(2)}) async-start(f32[1,32,128,128]{3,1,0,2:T(8,128)} %copy.56), calls=%async_computation.2 | async-start | bytes 4194304 | tf_op jit(solution)/shard_map/all_to_all | solution.py:67
  230.7 28.9 %all-to-all-start = ((f32[1,32,128,128]{3,1,0,2:T(8,128)}), f32[1,32,128,128]{3,1,0,2:T(8,128)}, u32[]{:S(2)}, u32[]{:S(2)}) async-start(f32[1,32,128,128]{3,1,0,2:T(8,128)} %copy.48), calls=%async_computation | async-start | bytes 4194304 | tf_op jit(solution)/shard_map/all_to_all | solution.py:67
  259.7 29.4 %all-to-all-start.4 = ((f32[1,32,128,128]{3,1,0,2:T(8,128)}), f32[1,32,128,128]{3,1,0,2:T(8,128)}, u32[]{:S(2)}, u32[]{:S(2)}) async-start(f32[1,32,128,128]{3,1,0,2:T(8,128)} %copy.64), calls=%async_computation.4 | async-start | bytes 4194304 | tf_op jit(solution)/shard_map/all_to_all | solution.py:67
  289.0 29.0 %all-to-all-start.6 = ((f32[1,32,128,128]{3,1,0,2:T(8,128)}), f32[1,32,128,128]{3,1,0,2:T(8,128)}, u32[]{:S(2)}, u32[]{:S(2)}) async-start(f32[1,32,128,128]{3,1,0,2:T(8,128)} %copy.72), calls=%async_computation.6 | async-start | bytes 4194304 | tf_op jit(solution)/shard_map/all_to_all | solution.py:67
  318.0 29.1 %all-to-all-start.3 = ((f32[1,128,32,128]{3,2,0,1:T(8,128)}), f32[1,128,32,128]{3,2,0,1:T(8,128)}, u32[]{:S(2)}, u32[]{:S(2)}) async-start(f32[1,128,32,128]{3,2,0,1:T(8,128)} %copy.60), calls=%async_computation.3 | async-start | bytes 4194304 | tf_op jit(solution)/shard_map/all_to_all | solution.py:72
  347.1 29.1 %all-to-all-start.1 = ((f32[1,128,32,128]{3,2,0,1:T(8,128)}), f32[1,128,32,128]{3,2,0,1:T(8,128)}, u32[]{:S(2)}, u32[]{:S(2)}) async-start(f32[1,128,32,128]{3,2,0,1:T(8,128)} %copy.52), calls=%async_computation.1 | async-start | bytes 4194304 | tf_op jit(solution)/shard_map/all_to_all | solution.py:72
  376.3 29.4 %all-to-all-start.5 = ((f32[1,128,32,128]{3,2,0,1:T(8,128)}), f32[1,128,32,128]{3,2,0,1:T(8,128)}, u32[]{:S(2)}, u32[]{:S(2)}) async-start(f32[1,128,32,128]{3,2,0,1:T(8,128)} %copy.68), calls=%async_computation.5 | async-start | bytes 4194304 | tf_op jit(solution)/shard_map/all_to_all | solution.py:72
  405.7 28.9 %all-to-all-start.7 = ((f32[1,128,32,128]{3,2,0,1:T(8,128)}), f32[1,128,32,128]{3,2,0,1:T(8,128)}, u32[]{:S(2)}, u32[]{:S(2)}) async-start(f32[1,128,32,128]{3,2,0,1:T(8,128)} %copy.76), calls=%async_computation.7 | async-start | bytes 4194304 | tf_op jit(solution)/shard_map/all_to_all | solution.py:72
  410.8 2.2 copy-start.6
  413.0 3.5 copy-start.5
  434.6 4.4 copy-start.3
  434.6 4.4 copy-start.4
  436.6 2.4 copy-start.1
  436.6 2.4 copy-start.2
  447.8 50.4 %all-to-all-start.8 = ((f32[1,32,128,128]{3,1,0,2:T(8,128)}), f32[1,32,128,128]{3,1,0,2:T(8,128)}, u32[]{:S(2)}, u32[]{:S(2)}) async-start(f32[1,32,128,128]{3,1,0,2:T(8,128)} %copy.79), calls=%async_computation.8 | async-start | bytes 4194304 | tf_op jit(solution)/shard_map/all_to_all | solution.py:76
  498.2 53.6 %all-to-all-start.9 = ((f32[1,32,128,128]{3,1,0,2:T(8,128)}), f32[1,32,128,128]{3,1,0,2:T(8,128)}, u32[]{:S(2)}, u32[]{:S(2)}) async-start(f32[1,32,128,128]{3,1,0,2:T(8,128)} %copy.82), calls=%async_computation.9 | async-start | bytes 4194304 | tf_op jit(solution)/shard_map/all_to_all | solution.py:75
Sparse Core Ops, SparseCore 0:
  16.0 176.7 all-reduce.2
where the time goes:
time: 623 us; the launch traced here: 617 us
  waiting for transfers between devices  358 us (57%)
  matrix products  84 us (13%)
  starting transfers between devices  54.6 us (9%)
  local copies, waits for them, and re-layouts  52.8 us (8%)
  blocking collectives  42.1 us (7%)
  between operations  16.7 us (3%)
  other arithmetic  8.11 us (1%)
    psum x1, waiting for transfers between devices, spread_2(): return lax.psum(block, axis)  177 us
    all_to_all x4, waiting for transfers between devices, per_device(): lax.all_to_all(spectra, 'grid', split_axis=2, concat_axis=1, tiled=True)  59.4 us
    all_to_all x1, waiting for transfers between devices, per_device(): lax.all_to_all(terms, 'band', split_axis=2, concat_axis=0, tiled=True)  43 us
    all_to_all x1, waiting for transfers between devices, per_device(): lax.all_to_all(orbitals, 'band', split_axis=2, concat_axis=0, tiled=True)  42.7 us
    psum x1, blocking collectives, per_device(): intersection = lax.psum(partial_intersection, ('band', 'grid'))  42.1 us
    all_to_all x4, waiting for transfers between devices, per_device(): lax.all_to_all(filtered, 'grid', split_axis=1, concat_axis=2, tiled=True)  36.4 us
    dot_general x8, matrix products, plane_transform(): return jnp.einsum('bxyk,yj->bxjk', spread, table_y, precision=highest)  25.4 us
    dot_general x8, matrix products, plane_transform(): spread = jnp.einsum('bxyz,zk->bxyk', field, table_z, precision=highest)  24.9 us
  transfers between devices with their start and end apart: 11, of which 11 were waited for; matrix products, arithmetic and copies ran while one was open for 16% of the time, Pallas kernels for 0%

commit v1 on v0

--- a/solution.py
+++ b/solution.py
@@ -5,6 +5,20 @@
 from jax.sharding import PartitionSpec as P
 
 highest = lax.Precision.HIGHEST
+
+
+def runs_note(block_here, join_dim, view):
+    f_next = block_here.shape
+    odd = block_here.reshape(
+        *f_next[:join_dim], view, f_next[join_dim] // view, *f_next[join_dim + 1 :]
+    )
+    return jnp.moveaxis(odd, join_dim, 0)
+
+
+def arrange_pools(u, which_dim):
+    field_out = list(u.shape[1:])
+    field_out[which_dim] *= u.shape[0]
+    return jnp.moveaxis(u, 0, which_dim).reshape(field_out)
 
 
 def spread_2(block, axis, owner):
@@ -71,9 +85,21 @@
         terms = terms + source * plane_transform(
             lax.all_to_all(filtered, "grid", split_axis=1, concat_axis=2, tiled=True)
         )
+
+    def unite_trees(link_axis, work_x, my_data, local_values):
+        kept_arr = lax.psum(1, link_axis)
+        carry, u1 = (kept_arr, lax.axis_index(link_axis))
+        fresh = runs_note(local_values, work_x, carry)
+        rows = [fresh[u1]]
+        for d in tuple(range(1, carry)):
+            aux = fresh[u1 ^ d]
+            rows.append(lax.ppermute(aux, link_axis, [(j0, j0 ^ d) for j0 in range(carry)]))
+        fresh = jnp.stack(rows)[u1 ^ jnp.arange(carry)]
+        return arrange_pools(fresh, my_data)
+
     orbital_cols, term_cols = (
         lax.all_to_all(orbitals, "band", split_axis=2, concat_axis=0, tiled=True),
-        lax.all_to_all(terms, "band", split_axis=2, concat_axis=0, tiled=True),
+        unite_trees("band", 2, 0, terms),
     )
     flat_orbitals = orbital_cols.reshape(total_bands, -1)
     flat_terms = term_cols.reshape(total_bands, -1)

time: 623 us -> 604 us (0.970)
  waiting for transfers between devices: 358 us -> 350 us
    ppermute x0 -> x7, waiting for transfers between devices: none -> 71 us  [unite_trees(): lax.ppermute(aux, link_axis, [(j0, j0 ^ d) for j0 in range(carry)])]
    all_to_all x1 -> x0, waiting for transfers between devices: 43 us -> none  [per_device(): lax.all_to_all(terms, 'band', split_axis=2, concat_axis=0, tiled=True)]
    all_to_all x1, waiting for transfers between devices: 42.7 us -> 0.01 us  [per_device(): lax.all_to_all(orbitals, 'band', split_axis=2, concat_axis=0, tiled=True)]
    ppermute x0 -> x7, starting transfers between devices: none -> 7.61 us  [unite_trees(): lax.ppermute(aux, link_axis, [(j0, j0 ^ d) for j0 in range(carry)])]
    all_to_all x4, waiting for transfers between devices: 36.4 us -> 42.6 us  [per_device(): lax.all_to_all(filtered, 'grid', split_axis=1, concat_axis=2, tiled=True)]
  transfers between devices with their start and end apart: 11 -> 17, of which waited for: 11 -> 15; matrix products, arithmetic and copies ran while one was open for 16% -> 18% of each run, Pallas kernels for 0% -> 0%
where the time goes in v1:
time: 604 us; the launch traced here: 596 us
  waiting for transfers between devices  350 us (58%)
  matrix products  77.8 us (13%)
  starting transfers between devices  54.3 us (9%)
  local copies, waits for them, and re-layouts  50.5 us (8%)
  blocking collectives  38.4 us (6%)
  between operations  16.7 us (3%)
  other arithmetic  8.09 us (1%)
    psum x1, waiting for transfers between devices, spread_2(): return lax.psum(block, axis)  177 us
    ppermute x7, waiting for transfers between devices, unite_trees(): lax.ppermute(aux, link_axis, [(j0, j0 ^ d) for j0 in range(carry)])  71 us
    all_to_all x4, waiting for transfers between devices, per_device(): lax.all_to_all(spectra, 'grid', split_axis=2, concat_axis=1, tiled=True)  59.4 us
    all_to_all x4, waiting for transfers between devices, per_device(): lax.all_to_all(filtered, 'grid', split_axis=1, concat_axis=2, tiled=True)  42.6 us
    psum x1, blocking collectives, per_device(): intersection = lax.psum(partial_intersection, ('band', 'grid'))  38.4 us
    dot_general x8, matrix products, plane_transform(): spread = jnp.einsum('bxyz,zk->bxyk', field, table_z, precision=highest)  23.4 us
    all_to_all x4, starting transfers between devices, per_device(): lax.all_to_all(filtered, 'grid', split_axis=1, concat_axis=2, tiled=True)  21.3 us
    dot_general x8, matrix products, plane_transform(): return jnp.einsum('bxyk,yj->bxjk', spread, table_y, precision=highest)  21.2 us
  transfers between devices with their start and end apart: 17, of which 15 were waited for; matrix products, arithmetic and copies ran while one was open for 18% of the time, Pallas kernels for 0%

profile of v1, /device:TPU:10, one launch (start us, length us, event | category | flops | bytes accessed | tf_op | source)
XLA Modules:
  0.0 595.8 jit_solution(10612311255756654816)
XLA Ops:
  10.6 5.3 broadcast_select_fusion.3
  15.9 176.9 %all-reduce.3.cloned.1.call-done = (f32[1,32,128,128]{3,2,1,0:T(8,128)}, f32[1,32,128,128]{3,2,1,0:T(8,128)}, f32[1,32,128,128]{3,2,1,0:T(8,128)}, f32[1,32,128,128]{3,2,1,0:T(8,128)}) async-done(((f32[1,32,128,128]{3,2,1,0:T(8,128)}, f32[1,32,128,128]{3,2,1,0:T(8,128)}, f32[1,32,128,128]{3,2,1,0:T(8,128)}, f32[1,32,128,128]{3,2,1,0:T(8,128)}), (f32[1,32,128,128]{3,2,1,0:T(8,128)}, ...) | async-done | bytes 8388624 | tf_op jit(solution)/shard_map/psum | solution.py:26
  192.8 3.7 fusion.12
  201.3 5.2 all-to-all-start.2
  206.4 3.7 fusion.14
  214.9 15.9 %all-to-all-done.2 = f32[1,32,128,128]{3,1,0,2:T(8,128)} async-done(((f32[1,32,128,128]{3,1,0,2:T(8,128)}), f32[1,32,128,128]{3,1,0,2:T(8,128)}, u32[]{:S(2)}, u32[]{:S(2)}) %all-to-all-start.2) | async-done | bytes 2097184 | tf_op jit(solution)/shard_map/all_to_all | solution.py:81
  230.8 5.0 all-to-all-start
  235.8 3.7 fusion.10
  244.2 15.5 %all-to-all-done = f32[1,32,128,128]{3,1,0,2:T(8,128)} async-done(((f32[1,32,128,128]{3,1,0,2:T(8,128)}), f32[1,32,128,128]{3,1,0,2:T(8,128)}, u32[]{:S(2)}, u32[]{:S(2)}) %all-to-all-start) | async-done | bytes 2097184 | tf_op jit(solution)/shard_map/all_to_all | solution.py:81
  259.7 5.2 all-to-all-start.4
  265.0 3.7 fusion.8
  273.4 15.4 %all-to-all-done.4 = f32[1,32,128,128]{3,1,0,2:T(8,128)} async-done(((f32[1,32,128,128]{3,1,0,2:T(8,128)}), f32[1,32,128,128]{3,1,0,2:T(8,128)}, u32[]{:S(2)}, u32[]{:S(2)}) %all-to-all-start.4) | async-done | bytes 2097184 | tf_op jit(solution)/shard_map/all_to_all | solution.py:81
  288.9 5.1 all-to-all-start.6
  305.2 12.6 %all-to-all-done.6 = f32[1,32,128,128]{3,1,0,2:T(8,128)} async-done(((f32[1,32,128,128]{3,1,0,2:T(8,128)}), f32[1,32,128,128]{3,1,0,2:T(8,128)}, u32[]{:S(2)}, u32[]{:S(2)}) %all-to-all-start.6) | async-done | bytes 2097184 | tf_op jit(solution)/shard_map/all_to_all | solution.py:81
  317.9 5.4 all-to-all-start.3
  334.6 12.6 %all-to-all-done.3 = f32[1,128,32,128]{3,2,0,1:T(8,128)} async-done(((f32[1,128,32,128]{3,2,0,1:T(8,128)}), f32[1,128,32,128]{3,2,0,1:T(8,128)}, u32[]{:S(2)}, u32[]{:S(2)}) %all-to-all-start.3) | async-done | bytes 2097184 | tf_op jit(solution)/shard_map/all_to_all | solution.py:86
  347.2 5.2 all-to-all-start.1
  363.7 12.7 %all-to-all-done.1 = f32[1,128,32,128]{3,2,0,1:T(8,128)} async-done(((f32[1,128,32,128]{3,2,0,1:T(8,128)}), f32[1,128,32,128]{3,2,0,1:T(8,128)}, u32[]{:S(2)}, u32[]{:S(2)}) %all-to-all-start.1) | async-done | bytes 2097184 | tf_op jit(solution)/shard_map/all_to_all | solution.py:86
  376.4 5.2 all-to-all-start.5
  392.8 12.7 %all-to-all-done.5 = f32[1,128,32,128]{3,2,0,1:T(8,128)} async-done(((f32[1,128,32,128]{3,2,0,1:T(8,128)}), f32[1,128,32,128]{3,2,0,1:T(8,128)}, u32[]{:S(2)}, u32[]{:S(2)}) %all-to-all-start.5) | async-done | bytes 2097184 | tf_op jit(solution)/shard_map/all_to_all | solution.py:86
  405.5 5.4 all-to-all-start.7
  421.2 3.5 fusion.88
  430.3 4.6 all-to-all-done.7
  434.9 4.9 all-to-all-start.8
  459.0 21.9 %collective-permute-done.1 = f32[1,32,16,128]{3,2,1,0:T(8,128)S(1)} collective-permute-done((f32[1,32,16,128]{3,2,1,0:T(8,128)}, f32[1,32,16,128]{3,2,1,0:T(8,128)S(1)}, u32[]{:S(2)}, u32[]{:S(2)}) %collective-permute-start.1) | collective-permute-done | bytes 262176 | tf_op jit(solution)/shard_map/ppermute | solution.py:96
  482.4 3.6 collective-permute-done.2
  486.0 27.3 %collective-permute-done.3 = f32[1,32,16,128]{3,2,1,0:T(8,128)S(1)} collective-permute-done((f32[1,32,16,128]{3,2,1,0:T(8,128)S(1)}, f32[1,32,16,128]{3,2,1,0:T(8,128)S(1)}, u32[]{:S(2)}, u32[]{:S(2)}) %collective-permute-start.3) | collective-permute-done | bytes 262176 | tf_op jit(solution)/shard_map/ppermute | solution.py:96
  513.3 5.6 collective-permute-done.4
  518.9 8.2 %collective-permute-done.5 = f32[1,32,16,128]{3,2,1,0:T(8,128)S(1)} collective-permute-done((f32[1,32,16,128]{3,2,1,0:T(8,128)S(1)}, f32[1,32,16,128]{3,2,1,0:T(8,128)S(1)}, u32[]{:S(2)}, u32[]{:S(2)}) %collective-permute-start.5) | collective-permute-done | bytes 262176 | tf_op jit(solution)/shard_map/ppermute | solution.py:96
  527.1 4.5 collective-permute-done.6
  535.2 7.7 %fusion.59 = f32[8,8]{0,1:T(8,128)S(1)} fusion(f32[1,32,8,16,128]{4,1,3,2,0:T(8,128)} %bitcast.79, f32[8,32,16,128]{3,2,1,0:T(8,128)S(1)} %gather_fusion), kind=kOutput, calls=%fused_computation.54 | convolution fusion | flops 50331712 | bytes 4194560 | tf_op jit(solution)/shard_map/dot_general | solution.py:107
  542.9 38.4 %psum.39 = f32[8,8]{0,1:T(8,128)S(1)} all-reduce(f32[8,8]{0,1:T(8,128)S(1)} %fusion.59), channel_id=1, replica_groups=mesh['band'=8,'grid'=4] {'band','grid'}, use_global_device_ids=true, to_apply=%region_4.5 | all-reduce | flops 64 | bytes 512 | tf_op jit(solution)/shard_map/psum | solution.py:110
  (92 shorter events, 112.7 us)
Async XLA Ops:
  6.5 186.3 %all-reduce.3.cloned.1.call-start = ((), (), s32[]{:S(2)}) async-start(), calls=%async_computation.9 | async-start | bytes 16777216 | tf_op jit(solution)/shard_map/psum | solution.py:26
  15.9 176.9 %copy-start = (f32[1,32,128,128]{3,2,1,0:T(8,128)S(1)}, f32[1,32,128,128]{3,2,1,0:T(8,128)}, u32[]{:S(2)}) copy-start(f32[1,32,128,128]{3,2,1,0:T(8,128)} %param.2) | copy-start | bytes 6291460
  201.3 29.5 %all-to-all-start.2 = ((f32[1,32,128,128]{3,1,0,2:T(8,128)}), f32[1,32,128,128]{3,1,0,2:T(8,128)}, u32[]{:S(2)}, u32[]{:S(2)}) async-start(f32[1,32,128,128]{3,1,0,2:T(8,128)} %copy.55), calls=%async_computation.2 | async-start | bytes 4194304 | tf_op jit(solution)/shard_map/all_to_all | solution.py:81
  230.8 29.0 %all-to-all-start = ((f32[1,32,128,128]{3,1,0,2:T(8,128)}), f32[1,32,128,128]{3,1,0,2:T(8,128)}, u32[]{:S(2)}, u32[]{:S(2)}) async-start(f32[1,32,128,128]{3,1,0,2:T(8,128)} %copy.47), calls=%async_computation | async-start | bytes 4194304 | tf_op jit(solution)/shard_map/all_to_all | solution.py:81
  259.7 29.1 %all-to-all-start.4 = ((f32[1,32,128,128]{3,1,0,2:T(8,128)}), f32[1,32,128,128]{3,1,0,2:T(8,128)}, u32[]{:S(2)}, u32[]{:S(2)}) async-start(f32[1,32,128,128]{3,1,0,2:T(8,128)} %copy.63), calls=%async_computation.4 | async-start | bytes 4194304 | tf_op jit(solution)/shard_map/all_to_all | solution.py:81
  288.9 29.0 %all-to-all-start.6 = ((f32[1,32,128,128]{3,1,0,2:T(8,128)}), f32[1,32,128,128]{3,1,0,2:T(8,128)}, u32[]{:S(2)}, u32[]{:S(2)}) async-start(f32[1,32,128,128]{3,1,0,2:T(8,128)} %copy.71), calls=%async_computation.6 | async-start | bytes 4194304 | tf_op jit(solution)/shard_map/all_to_all | solution.py:81
  317.9 29.3 %all-to-all-start.3 = ((f32[1,128,32,128]{3,2,0,1:T(8,128)}), f32[1,128,32,128]{3,2,0,1:T(8,128)}, u32[]{:S(2)}, u32[]{:S(2)}) async-start(f32[1,128,32,128]{3,2,0,1:T(8,128)} %copy.59), calls=%async_computation.3 | async-start | bytes 4194304 | tf_op jit(solution)/shard_map/all_to_all | solution.py:86
  347.2 29.2 %all-to-all-start.1 = ((f32[1,128,32,128]{3,2,0,1:T(8,128)}), f32[1,128,32,128]{3,2,0,1:T(8,128)}, u32[]{:S(2)}, u32[]{:S(2)}) async-start(f32[1,128,32,128]{3,2,0,1:T(8,128)} %copy.51), calls=%async_computation.1 | async-start | bytes 4194304 | tf_op jit(solution)/shard_map/all_to_all | solution.py:86
  376.4 29.2 %all-to-all-start.5 = ((f32[1,128,32,128]{3,2,0,1:T(8,128)}), f32[1,128,32,128]{3,2,0,1:T(8,128)}, u32[]{:S(2)}, u32[]{:S(2)}) async-start(f32[1,128,32,128]{3,2,0,1:T(8,128)} %copy.67), calls=%async_computation.5 | async-start | bytes 4194304 | tf_op jit(solution)/shard_map/all_to_all | solution.py:86
  405.5 29.3 %all-to-all-start.7 = ((f32[1,128,32,128]{3,2,0,1:T(8,128)}), f32[1,128,32,128]{3,2,0,1:T(8,128)}, u32[]{:S(2)}, u32[]{:S(2)}) async-start(f32[1,128,32,128]{3,2,0,1:T(8,128)} %copy.75), calls=%async_computation.7 | async-start | bytes 4194304 | tf_op jit(solution)/shard_map/all_to_all | solution.py:86
  434.9 100.4 %all-to-all-start.8 = ((f32[1,32,128,128]{3,1,0,2:T(8,128)}), f32[1,32,128,128]{3,1,0,2:T(8,128)}, u32[]{:S(2)}, u32[]{:S(2)}) async-start(f32[1,32,128,128]{3,1,0,2:T(8,128)} %copy.78), calls=%async_computation.8 | async-start | bytes 4194304 | tf_op jit(solution)/shard_map/all_to_all | solution.py:101
  442.0 6.4 %copy-start.5 = (f32[128,32,128]{2,0,1:T(8,128)S(1)}, f32[128,32,128]{2,0,1:T(8,128)}, u32[]{:S(2)}) copy-start(f32[128,32,128]{2,0,1:T(8,128)} %fusion.88) | copy-start | bytes 6291460
  442.0 6.4 %copy-start.6 = (f32[128,32,128]{2,0,1:T(8,128)S(1)}, f32[128,32,128]{2,0,1:T(8,128)}, u32[]{:S(2)}) copy-start(f32[128,32,128]{2,0,1:T(8,128)} %fusion.93) | copy-start | bytes 6291460
  443.9 4.4 copy-start.3
  443.9 4.4 copy-start.4
  446.1 2.2 copy-start.1
  446.2 2.3 copy-start.2
  452.8 4.7 collective-permute-start
  452.9 27.9 %collective-permute-start.1 = (f32[1,32,16,128]{3,2,1,0:T(8,128)}, f32[1,32,16,128]{3,2,1,0:T(8,128)S(1)}, u32[]{:S(2)}, u32[]{:S(2)}) collective-permute-start(f32[1,32,16,128]{3,2,1,0:T(8,128)} %get-tuple-element.14), channel_id=1, source_target_pairs={{0,8},{4,12},{8,0},{12,4},{16,24},{20,28},{24,16},{28,20},{1,9},{5... | collective-permute-start | bytes 786440 | tf_op jit(solution)/shard_map/ppermute | solution.py:96
  453.4 32.6 %collective-permute-start.2 = (f32[1,32,16,128]{3,2,1,0:T(8,128)}, f32[1,32,16,128]{3,2,1,0:T(8,128)S(1)}, u32[]{:S(2)}, u32[]{:S(2)}) collective-permute-start(f32[1,32,16,128]{3,2,1,0:T(8,128)} %get-tuple-element.13), channel_id=1, source_target_pairs={{0,12},{4,8},{8,4},{12,0},{16,28},{20,24},{24,20},{28,16},{1,13},{... | collective-permute-start | bytes 786440 | tf_op jit(solution)/shard_map/ppermute | solution.py:96
  454.8 58.5 %collective-permute-start.3 = (f32[1,32,16,128]{3,2,1,0:T(8,128)S(1)}, f32[1,32,16,128]{3,2,1,0:T(8,128)S(1)}, u32[]{:S(2)}, u32[]{:S(2)}) collective-permute-start(f32[1,32,16,128]{3,2,1,0:T(8,128)S(1)} %get-tuple-element.12), channel_id=1, source_target_pairs={{0,16},{4,20},{8,24},{12,28},{16,0},{20,4},{24,8},{28,12},{1,17},{... | collective-permute-start | bytes 786440 | tf_op jit(solution)/shard_map/ppermute | solution.py:96
  457.2 61.7 %collective-permute-start.4 = (f32[1,32,16,128]{3,2,1,0:T(8,128)S(1)}, f32[1,32,16,128]{3,2,1,0:T(8,128)S(1)}, u32[]{:S(2)}, u32[]{:S(2)}) collective-permute-start(f32[1,32,16,128]{3,2,1,0:T(8,128)S(1)} %get-tuple-element.11), channel_id=1, source_target_pairs={{0,20},{4,16},{8,28},{12,24},{16,4},{20,0},{24,12},{28,8},{1,21},{... | collective-permute-start | bytes 786440 | tf_op jit(solution)/shard_map/ppermute | solution.py:96
  457.5 69.6 %collective-permute-start.5 = (f32[1,32,16,128]{3,2,1,0:T(8,128)S(1)}, f32[1,32,16,128]{3,2,1,0:T(8,128)S(1)}, u32[]{:S(2)}, u32[]{:S(2)}) collective-permute-start(f32[1,32,16,128]{3,2,1,0:T(8,128)S(1)} %get-tuple-element.10), channel_id=1, source_target_pairs={{0,24},{4,28},{8,16},{12,20},{16,8},{20,12},{24,0},{28,4},{1,25},{... | collective-permute-start | bytes 786440 | tf_op jit(solution)/shard_map/ppermute | solution.py:96
  480.8 50.8 %collective-permute-start.6 = (f32[1,32,16,128]{3,2,1,0:T(8,128)S(1)}, f32[1,32,16,128]{3,2,1,0:T(8,128)S(1)}, u32[]{:S(2)}, u32[]{:S(2)}) collective-permute-start(f32[1,32,16,128]{3,2,1,0:T(8,128)S(1)} %get-tuple-element.9), channel_id=1, source_target_pairs={{0,28},{4,24},{8,20},{12,16},{16,12},{20,8},{24,4},{28,0},{1,29},{... | collective-permute-start | bytes 786440 | tf_op jit(solution)/shard_map/ppermute | solution.py:96
  531.6 1.3 copy-start.7
Sparse Core Ops, SparseCore 0:
  16.1 176.7 all-reduce.2
